TPU v7x, 128 devices: a whole 4x4x4 slice. The times are simulated.
128 devices in a mesh: dp: 8 (over z, core), label: 16 (over x, y).
Axes of the slice: x: 4, y: 4, z: 4, core: 2. Of those that a mesh axis runs over, the one named last changes fastest.
Arguments:
- features: bfloat16 [262144, 768], P(('dp', 'label')), may hold values from -6 to 6
- inst_ids: int32 [2048, 4], P(('dp', 'label')), may hold values from 0 to 15
- lab_ids: int32 [2048, 4], P(('dp', 'label')), may hold values from 0 to 15
- counts: int32 [2048], P(('dp', 'label')), may hold values from 0 to 4, as said below
- block_bits: int32 [2048, 4, 128, 128], P(('dp', 'label')), may hold values 0 or 1
- centroids: bfloat16 [2048, 768], P('label'), may hold values from -40 to 40
Outputs:
- label_embed: bfloat16 [32768, 768], P(('dp', 'label'))
- membership: bfloat16 [32768, 2048], P(('dp', 'label'))
- targets: bfloat16 [262144, 768], P(('dp', 'label'))
Inputs may be any that keep to these rules, and one draw needn't show every extreme that they name: `lab_ids`: label block within the slot's label column. `counts`: in every draw one label column has all 4 slots used on every device.
All inputs are finite; a program needn't handle non-finite values. No bound on the sum of `block_bits` on one device may be relied on, other than what follows from the above.
Results may differ from a plain program's by a relative error of at most 0.008.
The roundings to bfloat16 on the way count: a program that leaves them out, or rounds other values in their place, can miss the bound.
Values may be sent and summed in bfloat16 or wider, within the bound.
No kernel may reach another device: no remote copies, remote signals or barrier semaphores. Data moves between devices by JAX's collectives and lax.ppermute only.
A program may use at most 128 MiB of HBM per device.

v0:
```python
import jax
import jax.numpy as jnp
from jax import lax
from jax.sharding import PartitionSpec as P

LB_DEV = 2
epsilon = 1e-05


def label_side(column_sums, centroids):
    embed32 = column_sums * lax.rsqrt(
        jnp.mean(column_sums * column_sums, axis=1, keepdims=True) + epsilon
    )
    label_embed = embed32.astype(jnp.bfloat16)
    all_rows = lax.all_gather(centroids, "label", axis=0, tiled=True)
    scores = jnp.einsum("rd,kd->rk", label_embed, all_rows, preferred_element_type=jnp.float32)
    row_peak = jnp.max(scores, axis=1, keepdims=True)
    lifted = jnp.exp(scores - row_peak)
    membership = (lifted / jnp.sum(lifted, axis=1, keepdims=True)).astype(jnp.bfloat16)
    mixed_rows = jnp.dot(membership, all_rows, preferred_element_type=jnp.float32)
    return (label_embed, membership, mixed_rows.astype(jnp.bfloat16))


def body(features, inst_ids, lab_ids, counts, block_bits, centroids):
    dest_count, slot_cap = inst_ids.shape
    block_size = block_bits.shape[-1]
    feat_width = features.shape[1]
    inst_blocks = features.reshape(-1, block_size, feat_width)
    gathered = inst_blocks[inst_ids]
    incidence = block_bits.astype(jnp.bfloat16)
    partials = jnp.einsum(
        "ncab,ncad->ncbd", incidence, gathered, preferred_element_type=jnp.float32
    ).astype(jnp.bfloat16)
    filled = jnp.arange(slot_cap)[None, :] < counts[:, None]
    tagged_ids = jnp.where(filled, lab_ids, -1)
    arrived, arrived_ids = (
        lax.all_to_all(partials, "label", split_axis=0, concat_axis=0, tiled=True),
        lax.all_to_all(tagged_ids, "label", split_axis=0, concat_axis=0, tiled=True),
    )
    share_rows = LB_DEV * block_size
    col_blocks = lax.axis_size("dp") * LB_DEV
    slot_total = dest_count * slot_cap
    flat_ids = arrived_ids.reshape(slot_total)
    selector = (flat_ids[None, :] == jnp.arange(col_blocks)[:, None]).astype(jnp.bfloat16)
    column_sums = jnp.dot(
        selector,
        arrived.reshape(slot_total, block_size * feat_width),
        preferred_element_type=jnp.float32,
    )
    column_total = lax.psum(column_sums, "dp")
    embed_all, member_all, column_mixed = label_side(
        column_total.reshape(col_blocks * block_size, feat_width), centroids
    )
    offset = lax.axis_index("dp") * share_rows
    label_embed = lax.dynamic_slice_in_dim(embed_all, offset, share_rows, 0)
    membership = lax.dynamic_slice_in_dim(member_all, offset, share_rows, 0)
    mixed_blocks = column_mixed.reshape(col_blocks, block_size, feat_width)
    picked = mixed_blocks[jnp.maximum(arrived_ids, 0)]
    picked = jnp.where((arrived_ids >= 0)[:, :, None, None], picked, jnp.zeros_like(picked))
    returned = lax.all_to_all(picked, "label", split_axis=0, concat_axis=0, tiled=True)
    contrib = jnp.einsum("ncab,ncbd->ncad", incidence, returned, preferred_element_type=jnp.float32)
    owner_map = (
        inst_ids.reshape(slot_total)[None, :] == jnp.arange(inst_blocks.shape[0])[:, None]
    ).astype(jnp.float32)
    raw_targets = jnp.dot(
        owner_map,
        contrib.reshape(slot_total, block_size * feat_width),
        precision=lax.Precision.HIGHEST,
    )
    raw_targets = raw_targets.reshape(-1, feat_width)
    targets = raw_targets * lax.rsqrt(
        jnp.mean(raw_targets * raw_targets, axis=1, keepdims=True) + epsilon
    )
    return (label_embed, membership, targets.astype(jnp.bfloat16))


def solution(mesh):
    in_specs = (
        P(("dp", "label"), None),
        P(("dp", "label"), None),
        P(("dp", "label"), None),
        P(("dp", "label")),
        P(("dp", "label"), None, None, None),
        P("label", None),
    )
    out_specs = (P(("dp", "label"), None), P(("dp", "label"), None), P(("dp", "label"), None))
    return jax.shard_map(body, mesh=mesh, in_specs=in_specs, out_specs=out_specs, check_vma=False)
```

profile of v0, /device:TPU:61, one launch (start us, length us, event | category | flops | bytes accessed | tf_op | source)
XLA Modules:
  0.0 778.2 jit_solution(7269517425034337055)
XLA Ops:
  8.0 0.0 copy-start
  8.0 0.8 select_bitcast_fusion
  8.9 0.7 copy.27
  9.5 6.6 all-to-all-start
  16.1 0.7 compare_select_fusion
  16.8 0.1 copy.28
  16.9 0.1 reshape.75
  17.0 0.0 copy-done
  17.0 7.3 gather_fusion
  24.3 10.8 %convert_bitcast_fusion = bf16[16,4,128,768]{2,3,1,0:T(8,128)(2,1)} fusion(bf16[16,4,128,768]{3,2,1,0:T(8,128)(2,1)} %bitcast.31, s32[16,4,128,128]{3,2,1,0:T(8,128)} %param.10), kind=kOutput, calls=%fused_computation.5 | convolution fusion | flops 1617952768 | bytes 29360128 | tf_op jit(solution)/shard_map/ncab,ncad->ncbd/dot_general | solution.py:31
  35.1 0.0 all-to-all-done
  35.1 6.7 all-to-all-start.1
  41.7 0.0 all-reduce.2.cloned.1.call-start
  41.8 0.5 broadcast.82
  42.3 0.7 maximum_reduce_fusion
  43.0 0.1 eq.30
  43.1 219.6 %all-to-all-done.1 = bf16[16,4,128,768]{2,3,1,0:T(8,128)(2,1)} async-done(((bf16[16,4,128,768]{2,3,1,0:T(8,128)(2,1)}), bf16[16,4,128,768]{2,3,1,0:T(8,128)(2,1)}, u32[]{:S(2)}, u32[]{:S(2)}) %all-to-all-start.1) | async-done | bytes 12582944 | tf_op jit(solution)/shard_map/all_to_all | solution.py:37
  262.7 16.7 %copy.37 = bf16[8,8,128,768]{3,1,2,0:T(8,128)(2,1)} copy(bf16[8,8,128,768]{2,3,1,0:T(8,128)(2,1)} %bitcast.18) | data formatting | bytes 25165824
  279.4 9.0 %fusion.3 = f32[16,98304]{1,0:T(8,128)} fusion(bf16[64,98304]{1,0:T(8,128)(2,1)} %bitcast.34, s32[64]{0:T(128)S(1)} %eq.30), kind=kOutput, calls=%fused_computation.20 | convolution fusion | flops 201327616 | bytes 18874624 | tf_op jit(solution)/shard_map/dot_general | solution.py:45
  288.4 5.0 reshape.69
  293.4 0.0 all-reduce.2.cloned.1.call-update
  293.4 0.0 all-gather.2.cloned.1.call-start
  293.5 0.5 all-gather.2.cloned.1.call-update
  294.0 0.1 reshape.83
  294.1 0.1 copy.32
  294.2 0.1 copy.33
  294.3 91.9 %all-reduce.2.cloned.1.call-done = f32[2048,768]{1,0:T(8,128)} async-done(((f32[2048,768]{1,0:T(8,128)}), f32[2048,768]{1,0:T(8,128)}) %all-reduce.2.cloned.1.call-update) | async-done | bytes 6291472 | tf_op jit(solution)/shard_map/psum | solution.py:50
  386.2 0.0 copy-start.3
  386.2 3.4 multiply_reduce_fusion.1
  389.6 1.2 copy-done.3
  390.8 0.4 multiply_convert_fusion.1
  391.2 0.0 copy-start.5
  391.2 0.0 all-gather.2.cloned.1.call-done
  391.2 13.1 %fusion.7 = (f32[2048]{0:T(1024)S(1)}, f32[2048,2048]{0,1:T(8,128)}) fusion(bf16[2048,768]{1,0:T(8,128)(2,1)S(1)} %multiply_convert_fusion.1, bf16[2048,768]{1,0:T(8,128)(2,1)} %all-gather.2.cloned.1.call-done), kind=kOutput, calls=%fused_computation.32 | convolution fusion | flops 6446643200 | bytes 23076864 | tf_op jit(solution)/shard_map/rd,kd->rk/dot_general | solution.py:16
  404.4 0.0 copy-done.5
  404.4 8.1 %fusion = f32[2048]{0:T(1024)S(1)} fusion(f32[2048,2048]{0,1:T(8,128)} %get-tuple-element.15, f32[2048]{0:T(1024)S(1)} %get-tuple-element.14), kind=kLoop, calls=%fused_computation.4 | loop fusion | flops 8386560 | bytes 16793600 | tf_op jit(solution)/shard_map/reduce_sum | solution.py:19
  412.4 0.0 copy-start.7
  412.4 7.5 divide_convert_fusion
  419.9 0.0 copy-done.7
  419.9 0.0 copy-start.4
  419.9 7.3 convolution_convert_fusion
  427.2 0.0 copy-done.4
  427.3 7.1 gather_fusion.1
  434.4 16.6 %copy.34 = bf16[64,128,768]{1,2,0:T(8,128)(2,1)} copy(bf16[64,128,768]{2,1,0:T(8,128)(2,1)} %gather_fusion.1) | data formatting | bytes 25165824 | tf_op jit(solution)/shard_map/gather | solution.py:58
  451.0 10.6 %broadcast_select_fusion = bf16[16,4,128,768]{2,3,1,0:T(8,128)(2,1)} fusion(bf16[16,4,128,768]{2,3,1,0:T(8,128)(2,1)} %bitcast.32, pred[16,4]{1,0:T(8,128)(4,1)S(1)} %copy.33), kind=kLoop, calls=%fused_computation.6 | loop fusion | flops 6291456 | bytes 25165888 | tf_op jit(solution)/shard_map/jit(_where)/select_n | solution.py:59
  461.7 0.0 copy-start.6
  461.7 6.9 all-to-all-start.2
  468.5 0.0 copy-done.6
  468.5 0.1 copy.31
  468.6 0.1 eq.34
  468.7 1.3 constant_dynamic-slice_fusion
  470.0 1.4 copy.36
  471.4 1.8 constant_dynamic-slice_fusion.1
  473.2 232.2 %all-to-all-done.2 = bf16[16,4,128,768]{2,3,1,0:T(8,128)(2,1)} async-done(((bf16[16,4,128,768]{2,3,1,0:T(8,128)(2,1)}), bf16[16,4,128,768]{2,3,1,0:T(8,128)(2,1)}, u32[]{:S(2)}, u32[]{:S(2)}) %all-to-all-start.2) | async-done | bytes 12582944 | tf_op jit(solution)/shard_map/all_to_all | solution.py:60
  705.4 14.1 %convolution_bitcast_fusion = f32[16,4,128,768]{2,3,1,0:T(8,128)} fusion(bf16[16,4,128,768]{2,3,1,0:T(8,128)(2,1)} %all-to-all-done.2, s32[16,4,128,128]{3,2,1,0:T(8,128)} %param.10), kind=kOutput, calls=%fused_computation.7 | convolution fusion | flops 1611661312 | bytes 41943040 | tf_op jit(solution)/shard_map/ncab,ncbd->ncad/dot_general | solution.py:61
  719.5 25.1 %copy.38 = f32[8,8,128,768]{3,1,2,0:T(8,128)} copy(f32[8,8,128,768]{2,3,1,0:T(8,128)} %bitcast.29) | data formatting | bytes 50331648
  744.6 14.3 %fusion.4 = f32[16,98304]{1,0:T(8,128)} fusion(f32[64,98304]{1,0:T(8,128)} %bitcast.30, s32[64]{0:T(128)S(1)} %eq.34), kind=kOutput, calls=%fused_computation.21 | convolution fusion | flops 1207960576 | bytes 31457536 | tf_op jit(solution)/shard_map/dot_general | solution.py:65
  758.9 0.0 copy-start.1
  758.9 5.2 reshape.72
  764.1 0.0 copy-start.2
  764.1 3.4 multiply_reduce_fusion
  767.5 1.2 copy-done.2
  768.7 2.1 multiply_convert_fusion
  770.8 0.0 copy-done.1
  (5 shorter events, 0.0 us)
Async XLA Ops:
  8.0 9.0 %copy-start = (bf16[2048,768]{1,0:T(8,128)(2,1)S(1)}, bf16[2048,768]{1,0:T(8,128)(2,1)}, u32[]{:S(2)}) copy-start(bf16[2048,768]{1,0:T(8,128)(2,1)} %param.6) | copy-start | bytes 9437188
  9.5 25.5 %all-to-all-start = ((s32[16,1,4]{2,1,0:T(1,128)}), s32[16,1,4]{2,1,0:T(1,128)S(1)}, u32[]{:S(2)}, u32[]{:S(2)}) async-start(s32[16,1,4]{2,1,0:T(1,128)} %copy.27), calls=%async_computation | async-start | bytes 16384 | tf_op jit(solution)/shard_map/all_to_all | solution.py:38
  35.1 227.6 %all-to-all-start.1 = ((bf16[16,4,128,768]{2,3,1,0:T(8,128)(2,1)}), bf16[16,4,128,768]{2,3,1,0:T(8,128)(2,1)}, u32[]{:S(2)}, u32[]{:S(2)}) async-start(bf16[16,4,128,768]{2,3,1,0:T(8,128)(2,1)} %convert_bitcast_fusion), calls=%async_computation.1 | async-start | bytes 25165824 | tf_op jit(solution)/shard_map/all_to_all | solution.py:37
  41.7 344.4 %all-reduce.2.cloned.1.call-start = ((), (), s32[]{:S(2)}) async-start(), calls=%async_computation.3 | async-start | bytes 12582912 | tf_op jit(solution)/shard_map/psum | solution.py:50
  293.4 97.8 %all-gather.2.cloned.1.call-start = ((), (), s32[]{:S(2)}) async-start(), calls=%async_computation.4 | async-start | bytes 3342336 | tf_op jit(solution)/shard_map/all_gather | solution.py:15
  386.2 4.6 copy-start.3
  391.2 13.2 %copy-start.5 = (bf16[2048,768]{1,0:T(8,128)(2,1)}, bf16[2048,768]{1,0:T(8,128)(2,1)S(1)}, u32[]{:S(2)}) copy-start(bf16[2048,768]{1,0:T(8,128)(2,1)S(1)} %multiply_convert_fusion.1) | copy-start | bytes 9437188
  412.4 7.5 copy-start.7
  419.9 7.3 copy-start.4
  461.7 6.9 copy-start.6
  461.7 243.7 %all-to-all-start.2 = ((bf16[16,4,128,768]{2,3,1,0:T(8,128)(2,1)}), bf16[16,4,128,768]{2,3,1,0:T(8,128)(2,1)}, u32[]{:S(2)}, u32[]{:S(2)}) async-start(bf16[16,4,128,768]{2,3,1,0:T(8,128)(2,1)} %broadcast_select_fusion), calls=%async_computation.2 | async-start | bytes 25165824 | tf_op jit(solution)/shard_map/all_to_all | solution.py:60
  758.9 11.8 %copy-start.1 = (bf16[2048,768]{1,0:T(8,128)(2,1)S(1)}, bf16[2048,768]{1,0:T(8,128)(2,1)}, u32[]{:S(2)}) copy-start(bf16[2048,768]{1,0:T(8,128)(2,1)} %param.6) | copy-start | bytes 9437188
  764.1 4.6 copy-start.2
Sparse Core Ops, SparseCore 0:
  293.5 92.5 all-reduce.1
Sparse Core Ops, SparseCore 1:
  296.1 53.1 all-gather.1
where the time goes:
time: 780 us; the launch traced here: 778 us
  waiting for transfers between devices  544 us (70%)
  local copies, waits for them, and re-layouts  91.8 us (12%)
  matrix products  68.7 us (9%)
  other arithmetic  37.7 us (5%)
  starting transfers between devices  20.2 us (3%)
  between operations  15.6 us (2%)
    all_to_all x1, waiting for transfers between devices, body(): lax.all_to_all(picked, 'label', split_axis=0, concat_axis=0, tiled=True)  232 us
    all_to_all x1, waiting for transfers between devices, body(): lax.all_to_all(partials, 'label', split_axis=0, concat_axis=0, tiled=True)  220 us
    psum x1, waiting for transfers between devices, body(): column_total = lax.psum(column_sums, 'dp')  91.9 us
    unnamed x20, local copies, waits for them, and re-layouts  45.7 us
    gather x2, local copies, waits for them, and re-layouts, body(): picked = mixed_blocks[jnp.maximum(arrived_ids, 0)]  23.8 us
  transfers between devices with their start and end apart: 5, of which 3 were waited for; matrix products, arithmetic and copies ran while one was open for 4% of the time, Pallas kernels for 0%

commit v1 on v0

--- a/solution.py
+++ b/solution.py
@@ -47,7 +47,11 @@
         arrived.reshape(slot_total, block_size * feat_width),
         preferred_element_type=jnp.float32,
     )
-    column_total = lax.psum(column_sums, "dp")
+    column_total = column_sums
+    for hop in (1, 2, 4):
+        column_total = column_total + lax.ppermute(
+            column_total, "dp", [(dev, dev ^ hop) for dev in range(8)]
+        )
     embed_all, member_all, column_mixed = label_side(
         column_total.reshape(col_blocks * block_size, feat_width), centroids
     )

time: 780 us -> 977 us (1.25)
  waiting for transfers between devices: 544 us -> 713 us
  other arithmetic: 37.7 us -> 52.5 us
  starting transfers between devices: 20.2 us -> 30.6 us
    ppermute x0 -> x3, waiting for transfers between devices: none -> 281 us  [body(): lax.ppermute(column_total, 'dp', [(dev, dev ^ hop) for dev in range(8)])]
    psum x1 -> x0, waiting for transfers between devices: 91.9 us -> none  [body(): column_total = lax.psum(column_sums, 'dp')]
    all_to_all x1, waiting for transfers between devices: 232 us -> 212 us  [body(): lax.all_to_all(picked, 'label', split_axis=0, concat_axis=0, tiled=True)]
    add x0 -> x3, other arithmetic: none -> 14.7 us  [body(): column_total + lax.ppermute(column_total, 'dp', [(dev, dev ^ hop) for dev...]
  transfers between devices with their start and end apart: 5 -> 7, of which waited for: 3 -> 5; matrix products, arithmetic and copies ran while one was open for 4% -> 4% of each run, Pallas kernels for 0% -> 0%
where the time goes in v1:
time: 977 us; the launch traced here: 967 us
  waiting for transfers between devices  713 us (73%)
  local copies, waits for them, and re-layouts  91.9 us (9%)
  matrix products  65.3 us (7%)
  other arithmetic  52.5 us (5%)
  starting transfers between devices  30.6 us (3%)
  between operations  14.2 us (1%)
    ppermute x3, waiting for transfers between devices, body(): lax.ppermute(column_total, 'dp', [(dev, dev ^ hop) for dev in range(8)])  281 us
    all_to_all x1, waiting for transfers between devices, body(): lax.all_to_all(partials, 'label', split_axis=0, concat_axis=0, tiled=True)  220 us
    all_to_all x1, waiting for transfers between devices, body(): lax.all_to_all(picked, 'label', split_axis=0, concat_axis=0, tiled=True)  212 us
    unnamed x20, local copies, waits for them, and re-layouts  45.7 us
    gather x2, local copies, waits for them, and re-layouts, body(): picked = mixed_blocks[jnp.maximum(arrived_ids, 0)]  24 us
  transfers between devices with their start and end apart: 7, of which 5 were waited for; matrix products, arithmetic and copies ran while one was open for 4% of the time, Pallas kernels for 0%

profile of v1, /device:TPU:61, one launch (start us, length us, event | category | flops | bytes accessed | tf_op | source)
XLA Modules:
  0.0 967.1 jit_solution(12363704185281337248)
XLA Ops:
  7.2 0.0 copy-start
  7.2 0.8 select_bitcast_fusion
  8.0 0.7 copy.27
  8.7 6.6 all-to-all-start
  15.3 0.7 compare_select_fusion
  15.9 0.1 copy.28
  16.0 0.1 reshape.75
  16.1 0.0 copy-done
  16.1 7.3 gather_fusion
  23.4 10.7 %convert_bitcast_fusion = bf16[16,4,128,768]{2,3,1,0:T(8,128)(2,1)} fusion(bf16[16,4,128,768]{3,2,1,0:T(8,128)(2,1)} %bitcast.31, s32[16,4,128,128]{3,2,1,0:T(8,128)} %param.10), kind=kOutput, calls=%fused_computation.5 | convolution fusion | flops 1617952768 | bytes 29360128 | tf_op jit(solution)/shard_map/ncab,ncad->ncbd/dot_general | solution.py:31
  34.1 0.0 all-to-all-done
  34.1 6.7 all-to-all-start.1
  40.8 0.0 all-gather.2.cloned.1.call-start
  40.8 0.5 broadcast.82
  41.4 0.7 maximum_reduce_fusion
  42.1 0.1 eq.30
  42.1 219.5 %all-to-all-done.1 = bf16[16,4,128,768]{2,3,1,0:T(8,128)(2,1)} async-done(((bf16[16,4,128,768]{2,3,1,0:T(8,128)(2,1)}), bf16[16,4,128,768]{2,3,1,0:T(8,128)(2,1)}, u32[]{:S(2)}, u32[]{:S(2)}) %all-to-all-start.1) | async-done | bytes 12582944 | tf_op jit(solution)/shard_map/all_to_all | solution.py:37
  261.7 16.7 %copy.37 = bf16[8,8,128,768]{3,1,2,0:T(8,128)(2,1)} copy(bf16[8,8,128,768]{2,3,1,0:T(8,128)(2,1)} %bitcast.18) | data formatting | bytes 25165824
  278.4 5.6 fusion.3
  284.0 2.3 collective-permute-start
  286.3 9.9 %collective-permute-done = f32[16,98304]{1,0:T(8,128)} collective-permute-done((f32[16,98304]{1,0:T(8,128)S(1)}, f32[16,98304]{1,0:T(8,128)}, u32[]{:S(2)}, u32[]{:S(2)}) %collective-permute-start) | collective-permute-done | bytes 6291488 | tf_op jit(solution)/shard_map/ppermute | solution.py:52
  296.2 3.6 add.34
  299.7 0.1 collective-permute-start.1
  299.8 136.7 %collective-permute-done.1 = f32[16,98304]{1,0:T(8,128)S(1)} collective-permute-done((f32[16,98304]{1,0:T(8,128)S(1)}, f32[16,98304]{1,0:T(8,128)S(1)}, u32[]{:S(2)}, u32[]{:S(2)}) %collective-permute-start.1) | collective-permute-done | bytes 6291488 | tf_op jit(solution)/shard_map/ppermute | solution.py:52
  436.5 3.3 add.35
  439.8 2.8 collective-permute-start.2
  442.6 0.0 all-gather.2.cloned.1.call-update
  442.6 0.1 reshape.83
  442.7 0.1 copy.32
  442.8 0.1 copy.33
  442.9 134.6 %collective-permute-done.2 = f32[16,98304]{1,0:T(8,128)} collective-permute-done((f32[16,98304]{1,0:T(8,128)}, f32[16,98304]{1,0:T(8,128)}, u32[]{:S(2)}, u32[]{:S(2)}) %collective-permute-start.2) | collective-permute-done | bytes 6291488 | tf_op jit(solution)/shard_map/ppermute | solution.py:52
  577.5 7.9 add.36
  585.3 5.0 reshape.69
  590.3 3.4 multiply_reduce_fusion.1
  593.8 1.2 copy-done.2
  594.9 0.4 multiply_convert_fusion.1
  595.3 0.0 copy-start.5
  595.4 0.0 all-gather.2.cloned.1.call-done
  595.4 13.3 %fusion.7 = (f32[2048]{0:T(1024)S(1)}, f32[2048,2048]{0,1:T(8,128)}) fusion(bf16[2048,768]{1,0:T(8,128)(2,1)S(1)} %multiply_convert_fusion.1, bf16[2048,768]{1,0:T(8,128)(2,1)} %all-gather.2.cloned.1.call-done), kind=kOutput, calls=%fused_computation.32 | convolution fusion | flops 6446643200 | bytes 23076864 | tf_op jit(solution)/shard_map/rd,kd->rk/dot_general | solution.py:16
  608.7 0.0 copy-done.5
  608.7 8.1 fusion
  616.7 7.5 divide_convert_fusion
  624.2 0.0 copy-done.7
  624.2 0.0 copy-start.4
  624.2 7.3 convolution_convert_fusion
  631.6 0.0 copy-done.4
  631.6 7.3 gather_fusion.1
  638.9 16.7 %copy.34 = bf16[64,128,768]{1,2,0:T(8,128)(2,1)} copy(bf16[64,128,768]{2,1,0:T(8,128)(2,1)} %gather_fusion.1) | data formatting | bytes 25165824 | tf_op jit(solution)/shard_map/gather | solution.py:62
  655.6 10.7 %broadcast_select_fusion = bf16[16,4,128,768]{2,3,1,0:T(8,128)(2,1)} fusion(bf16[16,4,128,768]{2,3,1,0:T(8,128)(2,1)} %bitcast.32, pred[16,4]{1,0:T(8,128)(4,1)S(1)} %copy.33), kind=kLoop, calls=%fused_computation.6 | loop fusion | flops 6291456 | bytes 25165888 | tf_op jit(solution)/shard_map/jit(_where)/select_n | solution.py:63
  666.3 12.2 %all-to-all-start.2 = ((bf16[16,4,128,768]{2,3,1,0:T(8,128)(2,1)}), bf16[16,4,128,768]{2,3,1,0:T(8,128)(2,1)}, u32[]{:S(2)}, u32[]{:S(2)}) async-start(bf16[16,4,128,768]{2,3,1,0:T(8,128)(2,1)} %broadcast_select_fusion), calls=%async_computation.2 | async-start | bytes 25165824 | tf_op jit(solution)/shard_map/all_to_all | solution.py:64
  678.5 0.0 copy-done.6
  678.5 0.1 copy.31
  678.6 0.1 eq.34
  678.7 1.3 constant_dynamic-slice_fusion
  680.0 1.4 copy.36
  681.4 1.8 constant_dynamic-slice_fusion.1
  683.2 211.8 %all-to-all-done.2 = bf16[16,4,128,768]{2,3,1,0:T(8,128)(2,1)} async-done(((bf16[16,4,128,768]{2,3,1,0:T(8,128)(2,1)}), bf16[16,4,128,768]{2,3,1,0:T(8,128)(2,1)}, u32[]{:S(2)}, u32[]{:S(2)}) %all-to-all-start.2) | async-done | bytes 12582944 | tf_op jit(solution)/shard_map/all_to_all | solution.py:64
  895.0 14.1 %convolution_bitcast_fusion = f32[16,4,128,768]{2,3,1,0:T(8,128)} fusion(bf16[16,4,128,768]{2,3,1,0:T(8,128)(2,1)} %all-to-all-done.2, s32[16,4,128,128]{3,2,1,0:T(8,128)} %param.10), kind=kOutput, calls=%fused_computation.7 | convolution fusion | flops 1611661312 | bytes 41943040 | tf_op jit(solution)/shard_map/ncab,ncbd->ncad/dot_general | solution.py:65
  909.1 25.1 %copy.38 = f32[8,8,128,768]{3,1,2,0:T(8,128)} copy(f32[8,8,128,768]{2,3,1,0:T(8,128)} %bitcast.29) | data formatting | bytes 50331648
  934.3 14.3 %fusion.4 = f32[16,98304]{1,0:T(8,128)} fusion(f32[64,98304]{1,0:T(8,128)} %bitcast.30, s32[64]{0:T(128)S(1)} %eq.34), kind=kOutput, calls=%fused_computation.21 | convolution fusion | flops 1207960576 | bytes 31457536 | tf_op jit(solution)/shard_map/dot_general | solution.py:69
  948.6 5.0 reshape.72
  953.6 3.4 multiply_reduce_fusion
  957.0 1.2 copy-done.3
  958.2 2.1 multiply_convert_fusion
  (11 shorter events, 0.0 us)
Async XLA Ops:
  7.2 9.0 copy-start
  8.7 25.4 %all-to-all-start = ((s32[16,1,4]{2,1,0:T(1,128)}), s32[16,1,4]{2,1,0:T(1,128)S(1)}, u32[]{:S(2)}, u32[]{:S(2)}) async-start(s32[16,1,4]{2,1,0:T(1,128)} %copy.27), calls=%async_computation | async-start | bytes 16384 | tf_op jit(solution)/shard_map/all_to_all | solution.py:38
  34.1 227.5 %all-to-all-start.1 = ((bf16[16,4,128,768]{2,3,1,0:T(8,128)(2,1)}), bf16[16,4,128,768]{2,3,1,0:T(8,128)(2,1)}, u32[]{:S(2)}, u32[]{:S(2)}) async-start(bf16[16,4,128,768]{2,3,1,0:T(8,128)(2,1)} %convert_bitcast_fusion), calls=%async_computation.1 | async-start | bytes 25165824 | tf_op jit(solution)/shard_map/all_to_all | solution.py:37
  40.8 554.6 %all-gather.2.cloned.1.call-start = ((), (), s32[]{:S(2)}) async-start(), calls=%async_computation.3 | async-start | bytes 3342336 | tf_op jit(solution)/shard_map/all_gather | solution.py:15
  284.0 12.2 %collective-permute-start = (f32[16,98304]{1,0:T(8,128)S(1)}, f32[16,98304]{1,0:T(8,128)}, u32[]{:S(2)}, u32[]{:S(2)}) collective-permute-start(f32[16,98304]{1,0:T(8,128)S(1)} %fusion.3), channel_id=1, source_target_pairs={{0,16},{16,0},{32,48},{48,32},{64,80},{80,64},{96,112},{112,96},{1... | collective-permute-start | bytes 18874376 | tf_op jit(solution)/shard_map/ppermute | solution.py:52
  299.7 136.8 %collective-permute-start.1 = (f32[16,98304]{1,0:T(8,128)S(1)}, f32[16,98304]{1,0:T(8,128)S(1)}, u32[]{:S(2)}, u32[]{:S(2)}) collective-permute-start(f32[16,98304]{1,0:T(8,128)S(1)} %add.34), channel_id=1, source_target_pairs={{0,32},{16,48},{32,0},{48,16},{64,96},{80,112},{96,64},{112,80},{1... | collective-permute-start | bytes 18874376 | tf_op jit(solution)/shard_map/ppermute | solution.py:52
  439.8 137.7 %collective-permute-start.2 = (f32[16,98304]{1,0:T(8,128)}, f32[16,98304]{1,0:T(8,128)}, u32[]{:S(2)}, u32[]{:S(2)}) collective-permute-start(f32[16,98304]{1,0:T(8,128)} %add.35), channel_id=1, source_target_pairs={{0,64},{16,80},{32,96},{48,112},{64,0},{80,16},{96,32},{112,48},{1... | collective-permute-start | bytes 18874376 | tf_op jit(solution)/shard_map/ppermute | solution.py:52
  590.3 4.6 copy-start.2
  595.3 13.3 %copy-start.5 = (bf16[2048,768]{1,0:T(8,128)(2,1)}, bf16[2048,768]{1,0:T(8,128)(2,1)S(1)}, u32[]{:S(2)}) copy-start(bf16[2048,768]{1,0:T(8,128)(2,1)S(1)} %multiply_convert_fusion.1) | copy-start | bytes 9437188
  616.7 7.5 copy-start.7
  624.2 7.3 copy-start.4
  666.3 12.2 %copy-start.6 = (s32[16,4]{0,1:T(4,128)S(1)}, s32[16,4]{0,1:T(4,128)}, u32[]{:S(2)}) copy-start(s32[16,4]{0,1:T(4,128)} %param.7) | copy-start | bytes 772
  666.3 228.7 %all-to-all-start.2 = ((bf16[16,4,128,768]{2,3,1,0:T(8,128)(2,1)}), bf16[16,4,128,768]{2,3,1,0:T(8,128)(2,1)}, u32[]{:S(2)}, u32[]{:S(2)}) async-start(bf16[16,4,128,768]{2,3,1,0:T(8,128)(2,1)} %broadcast_select_fusion), calls=%async_computation.2 | async-start | bytes 25165824 | tf_op jit(solution)/shard_map/all_to_all | solution.py:64
  953.6 4.6 copy-start.3
  953.6 6.7 copy-start.1
Sparse Core Ops, SparseCore 0:
  442.7 50.6 all-gather.1
